TPU v7x, 256 devices: a whole 4x4x8 slice. The times are simulated.
256 devices in a mesh: ctx: 32 (over x, y, core), ch: 8 (over z).
Axes of the slice: x: 4, y: 4, z: 8, core: 2. Of those that a mesh axis runs over, the one named last changes fastest.
Arguments:
- gate_input: bfloat16 [8192, 16384], P('ch', 'ctx'), may hold values from -90 to 90
- key_input: bfloat16 [8192, 16384], P('ch', 'ctx'), may hold values from -6 to 6
- value_input: bfloat16 [8192, 16384], P('ch', 'ctx'), may hold values from -6 to 6
- short_filter: float32 [3, 3, 8192], P(None, None, 'ch'), may hold values from -3.5 to 3.5
- mr_filter: float32 [512, 128], P('ch'), may hold values from -0.5 to 0.5
- mr_skip: float32 [8192], P('ch'), may hold values from -3 to 3
- norm_gain: float32 [8192], P('ch'), may hold values from 0.5 to 1.5
- doc_lengths: int32 [64], replicated, may hold values from 1 to 2048, 16384 in all
Outputs:
- relaid: bfloat16 [8192, 16384], P(('ch', 'ctx'))
Inputs may be any that keep to these rules, and one draw needn't show every extreme that they name: `doc_lengths`: the 64 lengths sum to 16384, and one of them is exactly 2048.
All inputs are finite; a program needn't handle non-finite values.
Results may differ from a plain program's by a relative error of at most 0.0095.
Values may be sent and summed in bfloat16 or wider, within the bound.
No kernel may reach another device: no remote copies, remote signals or barrier semaphores. Data moves between devices by JAX's collectives and lax.ppermute only.
A program may use at most 128 MiB of HBM per device.

v0:
```python
import math
import jax
import jax.numpy as jnp
from jax import lax
from jax.sharding import PartitionSpec as P

D = 8192
GROUP = 16
SHORT = 3
MR = 128
NORM_EPS = 1e-06


def doc_starts(doc_lengths, positions):
    doc_ends = jnp.cumsum(doc_lengths)
    doc_firsts = doc_ends - doc_lengths
    before_row = doc_firsts[:, None] <= positions[None, :]
    return jnp.max(jnp.where(before_row, doc_firsts[:, None], 0), axis=0)


def short_conv(raw_rows, prior_rows, tap_rows, positions, starts):
    row_count = raw_rows.shape[1]
    extended = jnp.concatenate([prior_rows, raw_rows], axis=1).astype(jnp.float32)
    running = jnp.zeros(raw_rows.shape, jnp.float32)
    for tap_lag in range(SHORT):
        lagged = lax.slice_in_dim(
            extended, SHORT - 1 - tap_lag, SHORT - 1 - tap_lag + row_count, axis=1
        )
        in_document = positions - tap_lag >= starts
        running = running + jnp.where(
            in_document[None, :], tap_rows[tap_lag][:, None] * lagged, 0.0
        )
    return running


def features(raw_list, prior_list, short_taps, positions, starts):
    gate_conv = short_conv(raw_list[0], prior_list[0], short_taps[0], positions, starts)
    key_conv = short_conv(raw_list[1], prior_list[1], short_taps[1], positions, starts)
    value_conv = short_conv(raw_list[2], prior_list[2], short_taps[2], positions, starts)
    return (gate_conv, (key_conv * value_conv).astype(jnp.bfloat16))


def toeplitz(taps_bf):
    groups = taps_bf.shape[0]
    padded = jnp.concatenate(
        [jnp.zeros((groups, MR), jnp.bfloat16), taps_bf, jnp.zeros((groups, MR + 1), jnp.bfloat16)],
        axis=1,
    )
    repeated = jnp.tile(padded, (1, 2 * MR))[:, : 2 * MR * 3 * MR].reshape(groups, 2 * MR, 3 * MR)
    return repeated[:, :, 2 * MR :]


def long_conv(values, prior_rows, taps_bf, starts):
    channels, row_count = values.shape
    groups = taps_bf.shape[0]
    members = channels // groups
    tile_count = row_count // MR
    blocked = jnp.concatenate([prior_rows, values], axis=1).reshape(channels, tile_count + 1, MR)
    windows = jnp.concatenate([blocked[:, :-1], blocked[:, 1:]], axis=2).reshape(
        groups, members, tile_count, 2 * MR
    )
    matrices = toeplitz(taps_bf)
    per_step = math.gcd(tile_count, max(1, 64 // groups))
    tile_starts = starts.reshape(tile_count, MR)
    source_offsets = jnp.arange(2 * MR, dtype=jnp.int32) - MR
    step_offsets = jnp.arange(per_step, dtype=jnp.int32) * MR
    zero_bf = jnp.zeros((), jnp.bfloat16)

    def advance(step_index, result):
        block_begin = step_index * per_step
        window_part = lax.dynamic_slice_in_dim(windows, block_begin, per_step, axis=2)
        row_starts = lax.dynamic_slice_in_dim(tile_starts, block_begin, per_step, axis=0)
        tile_first = block_begin * MR + step_offsets
        sources = tile_first[:, None] + source_offsets[None, :]
        allowed = sources[:, :, None] >= row_starts[:, None, :]
        masked = jnp.where(allowed[:, None], matrices[None], zero_bf)
        product = jnp.einsum(
            "gcns,ngst->gcnt", window_part, masked, preferred_element_type=jnp.float32
        )
        return lax.dynamic_update_slice_in_dim(result, product, block_begin, axis=2)

    result = lax.fori_loop(
        0,
        tile_count // per_step,
        advance,
        jnp.zeros((groups, members, tile_count, MR), jnp.float32),
    )
    return result.reshape(channels, row_count)


def row_total(partial_value):
    return lax.psum(partial_value, "ch")


def local(
    gate_input, key_input, value_input, short_filter, mr_filter, mr_skip, norm_gain, doc_lengths
):
    ctx_place = lax.axis_index("ctx")
    stacked = jnp.stack([gate_input, key_input, value_input])
    received = lax.all_to_all(stacked, "ctx", split_axis=1, concat_axis=2, tiled=True)
    narrow = received.shape[1]
    all_rows = received.shape[2]
    chan_offset = ctx_place * narrow
    positions = jnp.arange(all_rows, dtype=jnp.int32)
    starts = doc_starts(doc_lengths, positions)
    short_taps = lax.dynamic_slice_in_dim(short_filter, chan_offset, narrow, axis=2)
    zero_prior = jnp.zeros((narrow, SHORT - 1), jnp.bfloat16)
    gate_conv, product_rows = features(
        [received[0], received[1], received[2]],
        [zero_prior, zero_prior, zero_prior],
        short_taps,
        positions,
        starts,
    )
    group_rows = lax.dynamic_slice_in_dim(
        mr_filter, chan_offset // GROUP, max(1, narrow // GROUP), axis=0
    )
    skip_here = lax.dynamic_slice_in_dim(mr_skip, chan_offset, narrow)
    gain_here = lax.dynamic_slice_in_dim(norm_gain, chan_offset, narrow)
    zero_rows = jnp.zeros((narrow, MR), jnp.bfloat16)
    mixed_rows = long_conv(
        product_rows, zero_rows, group_rows.astype(jnp.bfloat16), starts
    ) + skip_here[:, None] * product_rows.astype(jnp.float32)
    gated = gate_conv * mixed_rows
    shares = lax.psum_scatter(
        jnp.sum(gated * gated, axis=0).astype(jnp.bfloat16), "ctx", scatter_dimension=0, tiled=True
    ).astype(jnp.float32)
    own_scale = lax.rsqrt(row_total(shares) / D + NORM_EPS)
    row_scale = lax.all_gather(own_scale, "ctx", axis=0, tiled=True)
    return (gated * row_scale[None, :] * gain_here[:, None]).astype(jnp.bfloat16)


def solution(mesh):
    in_specs = (
        P("ch", "ctx"),
        P("ch", "ctx"),
        P("ch", "ctx"),
        P(None, None, "ch"),
        P("ch", None),
        P("ch"),
        P("ch"),
        P(),
    )
    out_specs = P(("ch", "ctx"), None)
    return jax.shard_map(local, mesh=mesh, in_specs=in_specs, out_specs=out_specs, check_vma=False)
```

profile of v0, /device:TPU:1, one launch (start us, length us, event | category | flops | bytes accessed | tf_op | source)
XLA Modules:
  0.0 279.0 jit_solution(16619326890867095155)
XLA Ops:
  0.0 2.2 pad_maximum_fusion
  2.2 4.7 %copy.30 = bf16[3,1024,512]{2,0,1:T(4,128)(2,1)} copy(bf16[3,1024,512]{2,1,0:T(8,128)(2,1)S(1)} %pad_maximum_fusion) | data formatting | bytes 6291456 | tf_op jit(solution)/shard_map/stack | solution.py:99
  6.9 8.8 %all-to-all-start = ((bf16[3,1024,512]{2,0,1:T(4,128)(2,1)}), bf16[3,1024,512]{2,0,1:T(4,128)(2,1)}, u32[]{:S(2)}, u32[]{:S(2)}) async-start(bf16[3,1024,512]{2,0,1:T(4,128)(2,1)} %copy.30), calls=%async_computation | async-start | bytes 8388608 | tf_op jit(solution)/shard_map/all_to_all | solution.py:100
  16.2 1.3 tile.10
  20.6 0.9 fusion.34
  21.5 0.8 select_reduce_fusion
  22.3 45.5 %all-to-all-done = bf16[3,1024,512]{2,0,1:T(4,128)(2,1)} async-done(((bf16[3,1024,512]{2,0,1:T(4,128)(2,1)}), bf16[3,1024,512]{2,0,1:T(4,128)(2,1)}, u32[]{:S(2)}, u32[]{:S(2)}) %all-to-all-start) | async-done | bytes 3145760 | tf_op jit(solution)/shard_map/all_to_all | solution.py:100
  67.9 11.2 %fusion.39 = (bf16[1,32,32,512]{3,0,1,2:T(2,128)(2,1)}, bf16[1,32,32,512]{3,0,1,2:T(2,128)(2,1)S(1)}, bf16[1,32,32,512]{3,0,1,2:T(2,128)(2,1)S(1)}) fusion(bf16[3,32,32,512]{3,0,1,2:T(4,128)(2,1)} %bitcast.6), kind=kLoop, calls=%fused_computation.77 | loop fusion | bytes 6291456 | tf_op jit(solution)/shard_map/slice | solution.py:109
  79.0 1.1 copy.33
  80.7 1.1 copy.32
  83.2 2.4 fusion.18
  87.1 1.6 broadcast_in_dim.159.clone
  88.7 15.0 %while.16 = (s32[]{:T(128)}, f32[2,16,128,128]{3,2,1,0:T(8,128)}, s32[128,128]{1,0:T(8,128)S(1)}, bf16[2,256,128]{2,1,0:T(8,128)(2,1)S(1)}, bf16[2,16,128,256]{3...) while((s32[]{:T(128)}, f32[2,16,128,128]{3,2,1,0:T(8,128)}, ...), condition=%wide.region_3.4_spmd.clone, body=%wide.region_2.3_spmd.clone.sunk | while | flops 70263112 | bytes 5491127 | solution.py:82
  88.8 1.4 broadcast_compare_fusion.2
  90.3 1.2 fusion.46
  91.5 1.0 copy_dynamic-update-slice_fusion.2
  92.5 1.4 broadcast_compare_fusion.2
  94.0 1.2 fusion.46
  95.2 1.0 copy_dynamic-update-slice_fusion.2
  96.3 1.4 broadcast_compare_fusion.2
  97.7 1.2 fusion.46
  98.9 1.0 copy_dynamic-update-slice_fusion.2
  100.0 1.4 broadcast_compare_fusion.2
  101.5 1.2 fusion.46
  102.7 1.0 copy_dynamic-update-slice_fusion.2
  103.7 2.7 copy.31
  107.4 1.2 copy-done.1
  108.6 2.3 multiply_reduce_fusion
  110.9 120.1 %all-reduce.4 = bf16[16384]{0:T(1024)(128)(2,1)S(1)} all-reduce(bf16[16384]{0:T(1024)(128)(2,1)S(1)} %get-tuple-element.225), channel_id=2, replica_groups=mesh['ctx'=32,'ch'=8] {'ctx'}, use_global_device_ids=true, to_apply=%region_5.6.clone | all-reduce | flops 16384 | bytes 65536
  231.1 16.5 %psum.7 = f32[512]{0:T(512)S(1)} all-reduce(f32[512]{0:T(512)S(1)} %dynamic-slice_convert_fusion), channel_id=1, replica_groups=mesh['ctx'=32,'ch'=8] {'ch'}, use_global_device_ids=true, to_apply=%region_6.7 | all-reduce | flops 512 | bytes 4096 | tf_op jit(solution)/shard_map/psum | solution.py:92
  247.6 30.2 %all-gather = f32[32,1,512]{2,1,0:T(1,128)S(1)} all-gather(f32[1,1,512]{2,1,0:T(1,128)S(1)} %bitcast.69), channel_id=1, replica_groups=mesh['ctx'=32,'ch'=8] {'ctx'}, dimensions={0}, use_global_device_ids=true | all-gather | bytes 67584 | tf_op jit(solution)/shard_map/all_gather | solution.py:129
  277.8 1.2 multiply_convert_fusion
  (56 shorter events, 7.8 us)
Async XLA Ops:
  0.0 16.1 %copy-start = (f32[64,128]{1,0:T(8,128)S(1)}, f32[64,128]{1,0:T(8,128)}, u32[]{:S(2)}) copy-start(f32[64,128]{1,0:T(8,128)} %param.14) | copy-start | bytes 98308
  6.9 8.8 %copy-start.2 = (s32[64]{0:T(128)S(1)}, s32[64]{0:T(128)}, u32[]{:S(2)}) copy-start(s32[64]{0:T(128)} %param.17) | copy-start | bytes 772
  6.9 61.0 %all-to-all-start = ((bf16[3,1024,512]{2,0,1:T(4,128)(2,1)}), bf16[3,1024,512]{2,0,1:T(4,128)(2,1)}, u32[]{:S(2)}, u32[]{:S(2)}) async-start(bf16[3,1024,512]{2,0,1:T(4,128)(2,1)} %copy.30), calls=%async_computation | async-start | bytes 8388608 | tf_op jit(solution)/shard_map/all_to_all | solution.py:100
  15.7 3.7 %copy-start.3 = (u32[256]{0:T(256)S(1)}, u32[256]{0:T(256)}, u32[]{:S(2)}) copy-start(u32[256]{0:T(256)} %constant.121) | copy-start | bytes 3076
  107.0 1.6 copy-start.1
where the time goes:
time: 279 us
  blocking collectives  167 us (60%)
  waiting for transfers between devices  45.5 us (16%)
  local copies, waits for them, and re-layouts  35.5 us (13%)
  other arithmetic  16.6 us (6%)
  starting transfers between devices  8.79 us (3%)
  matrix products  4.89 us (2%)
    unnamed x1, blocking collectives  120 us
    all_to_all x1, waiting for transfers between devices, local(): lax.all_to_all(stacked, 'ctx', split_axis=1, concat_axis=2, tiled=True)  45.5 us
    all_gather x1, blocking collectives, local(): row_scale = lax.all_gather(own_scale, 'ctx', axis=0, tiled=True)  30.2 us
    psum x1, blocking collectives, row_total(): return lax.psum(partial_value, 'ch')  16.5 us
    slice x2, local copies, waits for them, and re-layouts, local(): received[0]  13.9 us
    all_to_all x1, starting transfers between devices, local(): lax.all_to_all(stacked, 'ctx', split_axis=1, concat_axis=2, tiled=True)  8.79 us
  transfers between devices with their start and end apart: 1, of which 1 were waited for; matrix products, arithmetic and copies ran while one was open for 2% of the time, Pallas kernels for 0%

commit v1 on v0

--- a/solution.py
+++ b/solution.py
@@ -126,7 +126,9 @@
         jnp.sum(gated * gated, axis=0).astype(jnp.bfloat16), "ctx", scatter_dimension=0, tiled=True
     ).astype(jnp.float32)
     own_scale = lax.rsqrt(row_total(shares) / D + NORM_EPS)
-    row_scale = lax.all_gather(own_scale, "ctx", axis=0, tiled=True)
+    row_scale = jnp.concatenate(
+        lax.all_to_all(jnp.stack([own_scale] * lax.axis_size("ctx")), "ctx", 0, 0), axis=0
+    )
     return (gated * row_scale[None, :] * gain_here[:, None]).astype(jnp.bfloat16)
 
 

time: 279 us -> 270 us (0.968)
  blocking collectives: 167 us -> 137 us
  starting transfers between devices: 8.79 us -> 21.5 us
  waiting for transfers between devices: 45.5 us -> 53 us
    all_gather x1 -> x0, blocking collectives: 30.2 us -> none  [local(): row_scale = lax.all_gather(own_scale, 'ctx', axis=0, tiled=True)]
    all_to_all x0 -> x1, starting transfers between devices: none -> 12.7 us  [local(): lax.all_to_all(jnp.stack([own_scale] * lax.axis_size('ctx')), 'ctx', 0, 0)]
    all_to_all x0 -> x1, waiting for transfers between devices: none -> 6.71 us  [local(): lax.all_to_all(jnp.stack([own_scale] * lax.axis_size('ctx')), 'ctx', 0, 0)]
  transfers between devices with their start and end apart: 1 -> 2, of which waited for: 1 -> 2; matrix products, arithmetic and copies ran while one was open for 2% -> 2% of each run, Pallas kernels for 0% -> 0%
where the time goes in v1:
time: 270 us
  blocking collectives  137 us (51%)
  waiting for transfers between devices  53 us (20%)
  local copies, waits for them, and re-layouts  36.2 us (13%)
  starting transfers between devices  21.5 us (8%)
  other arithmetic  16.6 us (6%)
  matrix products  4.89 us (2%)
    unnamed x1, blocking collectives  120 us
    all_to_all x1, waiting for transfers between devices, local(): lax.all_to_all(stacked, 'ctx', split_axis=1, concat_axis=2, tiled=True)  46.3 us
    psum x1, blocking collectives, row_total(): return lax.psum(partial_value, 'ch')  16.5 us
    slice x2, local copies, waits for them, and re-layouts, local(): received[0]  13.9 us
    all_to_all x1, starting transfers between devices, local(): lax.all_to_all(jnp.stack([own_scale] * lax.axis_size('ctx')), 'ctx', 0, 0)  12.7 us
    all_to_all x1, starting transfers between devices, local(): lax.all_to_all(stacked, 'ctx', split_axis=1, concat_axis=2, tiled=True)  8.79 us
    all_to_all x1, waiting for transfers between devices, local(): lax.all_to_all(jnp.stack([own_scale] * lax.axis_size('ctx')), 'ctx', 0, 0)  6.71 us
    ge x4, other arithmetic, advance(): allowed = sources[:, :, None] >= row_starts[:, None, :]  5.57 us
  transfers between devices with their start and end apart: 2, of which 2 were waited for; matrix products, arithmetic and copies ran while one was open for 2% of the time, Pallas kernels for 0%

profile of v1, /device:TPU:1, one launch (start us, length us, event | category | flops | bytes accessed | tf_op | source)
XLA Modules:
  0.0 269.6 jit_solution(4944869704943773677)
XLA Ops:
  0.0 2.2 pad_maximum_fusion
  2.2 4.7 %copy.30 = bf16[3,1024,512]{2,0,1:T(4,128)(2,1)} copy(bf16[3,1024,512]{2,1,0:T(8,128)(2,1)S(1)} %pad_maximum_fusion) | data formatting | bytes 6291456 | tf_op jit(solution)/shard_map/stack | solution.py:99
  6.9 8.8 %all-to-all-start = ((bf16[3,1024,512]{2,0,1:T(4,128)(2,1)}), bf16[3,1024,512]{2,0,1:T(4,128)(2,1)}, u32[]{:S(2)}, u32[]{:S(2)}) async-start(bf16[3,1024,512]{2,0,1:T(4,128)(2,1)} %copy.30), calls=%async_computation | async-start | bytes 8388608 | tf_op jit(solution)/shard_map/all_to_all | solution.py:100
  16.2 1.3 tile.10
  19.8 0.9 fusion.34
  21.6 46.3 %all-to-all-done = bf16[3,1024,512]{2,0,1:T(4,128)(2,1)} async-done(((bf16[3,1024,512]{2,0,1:T(4,128)(2,1)}), bf16[3,1024,512]{2,0,1:T(4,128)(2,1)}, u32[]{:S(2)}, u32[]{:S(2)}) %all-to-all-start) | async-done | bytes 3145760 | tf_op jit(solution)/shard_map/all_to_all | solution.py:100
  67.9 11.2 %fusion.39 = (bf16[1,32,32,512]{3,0,1,2:T(2,128)(2,1)}, bf16[1,32,32,512]{3,0,1,2:T(2,128)(2,1)S(1)}, bf16[1,32,32,512]{3,0,1,2:T(2,128)(2,1)S(1)}) fusion(bf16[3,32,32,512]{3,0,1,2:T(4,128)(2,1)} %bitcast.6), kind=kLoop, calls=%fused_computation.77 | loop fusion | bytes 6291456 | tf_op jit(solution)/shard_map/slice | solution.py:109
  79.0 1.1 copy.33
  80.7 1.1 copy.32
  83.2 2.4 fusion.18
  87.1 1.6 broadcast_in_dim.158.clone
  88.7 15.0 %while.16 = (s32[]{:T(128)}, f32[2,16,128,128]{3,2,1,0:T(8,128)}, s32[128,128]{1,0:T(8,128)S(1)}, bf16[2,256,128]{2,1,0:T(8,128)(2,1)S(1)}, bf16[2,16,128,256]{3...) while((s32[]{:T(128)}, f32[2,16,128,128]{3,2,1,0:T(8,128)}, ...), condition=%wide.region_3.4_spmd.clone, body=%wide.region_2.3_spmd.clone.sunk | while | flops 70263112 | bytes 5491127 | solution.py:82
  88.8 1.4 broadcast_compare_fusion.2
  90.3 1.2 fusion.46
  91.5 1.0 copy_dynamic-update-slice_fusion.2
  92.5 1.4 broadcast_compare_fusion.2
  94.0 1.2 fusion.46
  95.2 1.0 copy_dynamic-update-slice_fusion.2
  96.3 1.4 broadcast_compare_fusion.2
  97.7 1.2 fusion.46
  98.9 1.0 copy_dynamic-update-slice_fusion.2
  100.0 1.4 broadcast_compare_fusion.2
  101.5 1.2 fusion.46
  102.7 1.0 copy_dynamic-update-slice_fusion.2
  103.7 2.7 %copy.31 = bf16[1,32,32,512]{3,2,1,0:T(8,128)(2,1)S(1)} copy(bf16[1,32,32,512]{3,0,1,2:T(2,128)(2,1)} %get-tuple-element.227) | data formatting | bytes 2097152 | tf_op jit(solution)/shard_map/slice | solution.py:109
  107.4 1.2 copy-done.1
  108.6 2.3 multiply_reduce_fusion
  110.9 120.1 %all-reduce.4 = bf16[16384]{0:T(1024)(128)(2,1)S(1)} all-reduce(bf16[16384]{0:T(1024)(128)(2,1)S(1)} %get-tuple-element.225), channel_id=2, replica_groups=mesh['ctx'=32,'ch'=8] {'ctx'}, use_global_device_ids=true, to_apply=%region_5.6.clone | all-reduce | flops 16384 | bytes 65536
  231.1 16.5 %psum.7 = f32[512]{0:T(512)S(1)} all-reduce(f32[512]{0:T(512)S(1)} %dynamic-slice_convert_fusion), channel_id=1, replica_groups=mesh['ctx'=32,'ch'=8] {'ch'}, use_global_device_ids=true, to_apply=%region_6.7 | all-reduce | flops 512 | bytes 4096 | tf_op jit(solution)/shard_map/psum | solution.py:92
  248.3 12.7 %all-to-all-start.1 = ((f32[32,1,512]{2,1,0:T(1,128)}), f32[32,1,512]{2,1,0:T(1,128)S(1)}, u32[]{:S(2)}, u32[]{:S(2)}) async-start(f32[32,1,512]{2,1,0:T(1,128)} %stack.14), calls=%async_computation.1 | async-start | bytes 131072 | tf_op jit(solution)/shard_map/all_to_all | solution.py:130
  261.7 6.7 %all-to-all-done.1 = f32[32,1,512]{2,1,0:T(1,128)S(1)} async-done(((f32[32,1,512]{2,1,0:T(1,128)}), f32[32,1,512]{2,1,0:T(1,128)S(1)}, u32[]{:S(2)}, u32[]{:S(2)}) %all-to-all-start.1) | async-done | bytes 65568 | tf_op jit(solution)/shard_map/all_to_all | solution.py:130
  268.4 1.2 multiply_convert_fusion
  (58 shorter events, 9.2 us)
Async XLA Ops:
  0.0 16.1 %copy-start = (f32[64,128]{1,0:T(8,128)S(1)}, f32[64,128]{1,0:T(8,128)}, u32[]{:S(2)}) copy-start(f32[64,128]{1,0:T(8,128)} %param.14) | copy-start | bytes 98308
  6.9 8.8 %copy-start.2 = (s32[64]{0:T(128)S(1)}, s32[64]{0:T(128)}, u32[]{:S(2)}) copy-start(s32[64]{0:T(128)} %param.17) | copy-start | bytes 772
  6.9 61.0 %all-to-all-start = ((bf16[3,1024,512]{2,0,1:T(4,128)(2,1)}), bf16[3,1024,512]{2,0,1:T(4,128)(2,1)}, u32[]{:S(2)}, u32[]{:S(2)}) async-start(bf16[3,1024,512]{2,0,1:T(4,128)(2,1)} %copy.30), calls=%async_computation | async-start | bytes 8388608 | tf_op jit(solution)/shard_map/all_to_all | solution.py:100
  15.7 3.0 %copy-start.3 = (u32[256]{0:T(256)S(1)}, u32[256]{0:T(256)}, u32[]{:S(2)}) copy-start(u32[256]{0:T(256)} %constant.121) | copy-start | bytes 3076
  107.0 1.6 copy-start.1
  248.3 20.2 %all-to-all-start.1 = ((f32[32,1,512]{2,1,0:T(1,128)}), f32[32,1,512]{2,1,0:T(1,128)S(1)}, u32[]{:S(2)}, u32[]{:S(2)}) async-start(f32[32,1,512]{2,1,0:T(1,128)} %stack.14), calls=%async_computation.1 | async-start | bytes 131072 | tf_op jit(solution)/shard_map/all_to_all | solution.py:130

commit v2 on v0

--- a/solution.py
+++ b/solution.py
@@ -89,7 +89,7 @@
 
 
 def row_total(partial_value):
-    return lax.psum(partial_value, "ch")
+    return jnp.sum(lax.all_gather(partial_value, "ch"), axis=0)
 
 
 def local(

time: 279 us -> 285 us (1.022)
  blocking collectives: 167 us -> 172 us
    all_gather x0 -> x1, blocking collectives: none -> 19.9 us  [row_total(): return jnp.sum(lax.all_gather(partial_value, 'ch'), axis=0)]
    psum x1 -> x0, blocking collectives: 16.5 us -> none  [row_total(): return lax.psum(partial_value, 'ch')]
where the time goes in v2:
time: 285 us; the launch traced here: 284 us
  blocking collectives  172 us (60%)
  waiting for transfers between devices  45.5 us (16%)
  local copies, waits for them, and re-layouts  35.5 us (12%)
  other arithmetic  16.6 us (6%)
  starting transfers between devices  8.79 us (3%)
  matrix products  4.89 us (2%)
    unnamed x1, blocking collectives  120 us
    all_to_all x1, waiting for transfers between devices, local(): lax.all_to_all(stacked, 'ctx', split_axis=1, concat_axis=2, tiled=True)  45.5 us
    all_gather x1, blocking collectives, local(): row_scale = lax.all_gather(own_scale, 'ctx', axis=0, tiled=True)  32.1 us
    all_gather x1, blocking collectives, row_total(): return jnp.sum(lax.all_gather(partial_value, 'ch'), axis=0)  19.9 us
    slice x2, local copies, waits for them, and re-layouts, local(): received[0]  13.9 us
    all_to_all x1, starting transfers between devices, local(): lax.all_to_all(stacked, 'ctx', split_axis=1, concat_axis=2, tiled=True)  8.79 us
  transfers between devices with their start and end apart: 1, of which 1 were waited for; matrix products, arithmetic and copies ran while one was open for 2% of the time, Pallas kernels for 0%

profile of v2, /device:TPU:1, one launch (start us, length us, event | category | flops | bytes accessed | tf_op | source)
XLA Modules:
  0.0 284.4 jit_solution(4545439141907128054)
XLA Ops:
  0.0 2.2 pad_maximum_fusion
  2.2 4.7 %copy.30 = bf16[3,1024,512]{2,0,1:T(4,128)(2,1)} copy(bf16[3,1024,512]{2,1,0:T(8,128)(2,1)S(1)} %pad_maximum_fusion) | data formatting | bytes 6291456 | tf_op jit(solution)/shard_map/stack | solution.py:99
  6.9 8.8 %all-to-all-start = ((bf16[3,1024,512]{2,0,1:T(4,128)(2,1)}), bf16[3,1024,512]{2,0,1:T(4,128)(2,1)}, u32[]{:S(2)}, u32[]{:S(2)}) async-start(bf16[3,1024,512]{2,0,1:T(4,128)(2,1)} %copy.30), calls=%async_computation | async-start | bytes 8388608 | tf_op jit(solution)/shard_map/all_to_all | solution.py:100
  16.2 1.3 tile.10
  20.6 0.9 fusion.34
  21.5 0.8 select_reduce_fusion
  22.3 45.5 %all-to-all-done = bf16[3,1024,512]{2,0,1:T(4,128)(2,1)} async-done(((bf16[3,1024,512]{2,0,1:T(4,128)(2,1)}), bf16[3,1024,512]{2,0,1:T(4,128)(2,1)}, u32[]{:S(2)}, u32[]{:S(2)}) %all-to-all-start) | async-done | bytes 3145760 | tf_op jit(solution)/shard_map/all_to_all | solution.py:100
  67.9 11.2 %fusion.39 = (bf16[1,32,32,512]{3,0,1,2:T(2,128)(2,1)}, bf16[1,32,32,512]{3,0,1,2:T(2,128)(2,1)S(1)}, bf16[1,32,32,512]{3,0,1,2:T(2,128)(2,1)S(1)}) fusion(bf16[3,32,32,512]{3,0,1,2:T(4,128)(2,1)} %bitcast.6), kind=kLoop, calls=%fused_computation.77 | loop fusion | bytes 6291456 | tf_op jit(solution)/shard_map/slice | solution.py:109
  79.0 1.1 copy.33
  80.7 1.1 copy.32
  83.2 2.4 fusion.18
  87.1 1.6 broadcast_in_dim.159.clone
  88.7 15.0 %while.16 = (s32[]{:T(128)}, f32[2,16,128,128]{3,2,1,0:T(8,128)}, s32[128,128]{1,0:T(8,128)S(1)}, bf16[2,256,128]{2,1,0:T(8,128)(2,1)S(1)}, bf16[2,16,128,256]{3...) while((s32[]{:T(128)}, f32[2,16,128,128]{3,2,1,0:T(8,128)}, ...), condition=%wide.region_3.4_spmd.clone, body=%wide.region_2.3_spmd.clone.sunk | while | flops 70263112 | bytes 5491127 | solution.py:82
  88.8 1.4 broadcast_compare_fusion.2
  90.3 1.2 fusion.46
  91.5 1.0 copy_dynamic-update-slice_fusion.2
  92.5 1.4 broadcast_compare_fusion.2
  94.0 1.2 fusion.46
  95.2 1.0 copy_dynamic-update-slice_fusion.2
  96.3 1.4 broadcast_compare_fusion.2
  97.7 1.2 fusion.46
  98.9 1.0 copy_dynamic-update-slice_fusion.2
  100.0 1.4 broadcast_compare_fusion.2
  101.5 1.2 fusion.46
  102.7 1.0 copy_dynamic-update-slice_fusion.2
  103.7 2.7 copy.31
  107.4 1.2 copy-done.1
  108.6 2.3 multiply_reduce_fusion
  110.9 120.1 %all-reduce.4 = bf16[16384]{0:T(1024)(128)(2,1)S(1)} all-reduce(bf16[16384]{0:T(1024)(128)(2,1)S(1)} %get-tuple-element.225), channel_id=3, replica_groups=mesh['ctx'=32,'ch'=8] {'ctx'}, use_global_device_ids=true, to_apply=%region_5.6.clone | all-reduce | flops 16384 | bytes 65536
  231.1 19.9 %all-gather.1 = f32[8,1,512]{2,1,0:T(1,128)S(1)} all-gather(f32[1,1,512]{2,1,0:T(1,128)S(1)} %bitcast.70), channel_id=2, replica_groups=mesh['ctx'=32,'ch'=8] {'ch'}, dimensions={0}, use_global_device_ids=true | all-gather | bytes 18432 | tf_op jit(solution)/shard_map/all_gather | solution.py:92
  251.1 32.1 %all-gather.2 = f32[32,1,512]{2,1,0:T(1,128)S(1)} all-gather(f32[1,1,512]{2,1,0:T(1,128)S(1)} %bitcast.71), channel_id=1, replica_groups=mesh['ctx'=32,'ch'=8] {'ctx'}, dimensions={0}, use_global_device_ids=true | all-gather | bytes 67584 | tf_op jit(solution)/shard_map/all_gather | solution.py:129
  283.2 1.2 multiply_convert_fusion
  (57 shorter events, 7.8 us)
Async XLA Ops:
  0.0 16.1 %copy-start = (f32[64,128]{1,0:T(8,128)S(1)}, f32[64,128]{1,0:T(8,128)}, u32[]{:S(2)}) copy-start(f32[64,128]{1,0:T(8,128)} %param.14) | copy-start | bytes 98308
  6.9 8.8 %copy-start.2 = (s32[64]{0:T(128)S(1)}, s32[64]{0:T(128)}, u32[]{:S(2)}) copy-start(s32[64]{0:T(128)} %param.17) | copy-start | bytes 772
  6.9 61.0 %all-to-all-start = ((bf16[3,1024,512]{2,0,1:T(4,128)(2,1)}), bf16[3,1024,512]{2,0,1:T(4,128)(2,1)}, u32[]{:S(2)}, u32[]{:S(2)}) async-start(bf16[3,1024,512]{2,0,1:T(4,128)(2,1)} %copy.30), calls=%async_computation | async-start | bytes 8388608 | tf_op jit(solution)/shard_map/all_to_all | solution.py:100
  15.7 3.7 %copy-start.3 = (u32[256]{0:T(256)S(1)}, u32[256]{0:T(256)}, u32[]{:S(2)}) copy-start(u32[256]{0:T(256)} %constant.121) | copy-start | bytes 3076
  107.0 1.6 copy-start.1
